TPU v7x, 128 devices: a whole 4x4x4 slice. The times are simulated.
128 devices in a mesh: agent: 8 (over z, core), chan: 8 (over y, x_hi), batch: 2 (over x_lo).
Axes of the slice: x: 4 (x_hi: 2, x_lo: 2; x = x_hi * 2 + x_lo), y: 4, z: 4, core: 2. Of those that a mesh axis runs over, the one named last changes fastest.
Arguments:
- features: bfloat16 [256, 16, 16384], P(None, None, ('agent', 'chan', 'batch')), may hold values from -6 to 6
- norm_gain: float32 [256], replicated, may hold values from 0.1 to 1.9
- tok_in: bfloat16 [16384, 2048], P('agent'), may hold values from -0.046875 to 0.046875
- tok_out: bfloat16 [2048, 16384], P(None, 'agent'), may hold values from -0.125 to 0.125
- mix_gain: float32 [256], replicated, may hold values from 0.1 to 1.9
- chan_in: bfloat16 [256, 1024], replicated, may hold values from -0.375 to 0.375
- chan_out: bfloat16 [1024, 256], replicated, may hold values from -0.1875 to 0.1875
- head: bfloat16 [256, 8], replicated, may hold values from -8 to 8
- actions: int32 [16, 16384], P(None, ('agent', 'chan', 'batch')), may hold values from 0 to 7
- order: int32 [16384], P(('agent', 'chan', 'batch')), may hold values from 0 to 16383, as said below
Outputs:
- input_grad: float32 [256, 16, 16384], P(None, None, ('agent', 'chan', 'batch'))
- head_grad: float32 [256, 8], replicated
Inputs may be any that keep to these rules, and one draw needn't show every extreme that they name: order maps each aligned block of 128 agents one to one onto the same block.
All inputs are finite; a program needn't handle non-finite values.
Results may differ from a plain program's by a relative error of at most 0.025.
Values may be sent and summed in bfloat16 or wider, within the bound.
A program may use at most 128 MiB of HBM per device.

v0:
```python
import jax
import jax.numpy as jnp
from jax import lax
from jax.sharding import PartitionSpec as P

A = 16384
GELU_K = 0.7978845608028654
GELU_C = 0.044715
EPS = 1e-05


def gelu_value(v):
    return 0.5 * v * (1.0 + jnp.tanh(GELU_K * (v + GELU_C * v * v * v)))


def gelu_slope(v):
    inner = jnp.tanh(GELU_K * (v + GELU_C * v * v * v))
    return 0.5 * (1.0 + inner) + 0.5 * v * (1.0 - inner * inner) * GELU_K * (
        1.0 + 3.0 * GELU_C * v * v
    )


def shaped_gain(gain, field):
    return gain.reshape((gain.shape[0],) + (1,) * (field.ndim - 1))


def norm_forward(field, gain):
    center = jnp.mean(field, axis=0, keepdims=True)
    spread = jnp.mean(jnp.square(field - center), axis=0, keepdims=True)
    scale = lax.rsqrt(spread + EPS)
    unit = (field - center) * scale
    return (unit * shaped_gain(gain, field), unit, scale)


def norm_backward(upstream, gain, unit, scale):
    weighted = upstream * shaped_gain(gain, upstream)
    return scale * (
        weighted
        - jnp.mean(weighted, axis=0, keepdims=True)
        - unit * jnp.mean(weighted * unit, axis=0, keepdims=True)
    )


def to_tokens(field):
    return lax.all_to_all(field, ("chan", "batch"), split_axis=0, concat_axis=2, tiled=True)


def to_channels(field):
    return lax.all_to_all(field, ("chan", "batch"), split_axis=2, concat_axis=0, tiled=True)


def project(weight, hidden_dim, rows):
    agent_dim = 1 - hidden_dim
    partial_sum = lax.dot_general(
        weight, rows, (((agent_dim,), (1,)), ((), ())), preferred_element_type=jnp.float32
    )
    return lax.psum(partial_sum, "agent")


def expand(spread, weight, hidden_dim):
    return lax.dot_general(
        spread, weight, (((0,), (hidden_dim,)), ((), ())), preferred_element_type=jnp.float32
    )


def shards(features, norm_gain, tok_in, tok_out, mix_gain, chan_in, chan_out, head, actions, order):
    wide = features.astype(jnp.float32)
    chans, samples, local = wide.shape
    normed_in, unit_in, scale_in = norm_forward(wide, norm_gain)
    spread_in = to_tokens(normed_in.astype(jnp.bfloat16))
    token_chans, _, agents = spread_in.shape
    token_rows = spread_in.reshape(token_chans * samples, agents)
    hidden_pre = project(tok_in, 1, token_rows)
    hidden_act = gelu_value(hidden_pre).astype(jnp.bfloat16)
    mixed = (
        expand(hidden_act, tok_out, 0).astype(jnp.bfloat16).reshape(token_chans, samples, agents)
    )
    mixed_back = to_channels(mixed)
    first = wide + mixed_back.astype(jnp.float32)
    normed_mid, unit_mid, scale_mid = norm_forward(first, mix_gain)
    flat_mid = normed_mid.astype(jnp.bfloat16).reshape(chans, samples * local)
    inner_pre = lax.dot_general(
        chan_in, flat_mid, (((0,), (0,)), ((), ())), preferred_element_type=jnp.float32
    )
    inner = gelu_value(inner_pre).astype(jnp.bfloat16)
    outer = lax.dot_general(
        chan_out, inner, (((0,), (0,)), ((), ())), preferred_element_type=jnp.float32
    )
    second = (first.reshape(chans, samples * local) + outer).astype(jnp.bfloat16)
    logits = lax.dot_general(
        head, second, (((0,), (0,)), ((), ())), preferred_element_type=jnp.float32
    )
    target = jnp.take_along_axis(actions, (order % local)[None, :], axis=1).reshape(
        1, samples * local
    )
    phases = lax.broadcasted_iota(jnp.int32, logits.shape, 0)
    picked = (phases == target).astype(jnp.float32)
    top = jnp.max(logits, axis=0, keepdims=True)
    exps = jnp.exp(logits - top)
    probs = exps / jnp.sum(exps, axis=0, keepdims=True)
    slope = (probs - picked).astype(jnp.bfloat16)
    head_part = lax.dot_general(
        second, slope, (((1,), (1,)), ((), ())), preferred_element_type=jnp.float32
    )
    head_total = lax.psum(head_part, ("agent", "chan", "batch"))
    head_grad = head_total * (1.0 / (samples * A))
    back_second = lax.dot_general(
        head, slope, (((1,), (0,)), ((), ())), preferred_element_type=jnp.float32
    )
    back_low = back_second.astype(jnp.bfloat16)
    back_inner = lax.dot_general(
        chan_out, back_low, (((1,), (0,)), ((), ())), preferred_element_type=jnp.float32
    )
    back_inner_pre = (back_inner * gelu_slope(inner_pre)).astype(jnp.bfloat16)
    back_mid = lax.dot_general(
        chan_in, back_inner_pre, (((1,), (0,)), ((), ())), preferred_element_type=jnp.float32
    )
    back_first = back_second.reshape(chans, samples, local) + norm_backward(
        back_mid.reshape(chans, samples, local), mix_gain, unit_mid, scale_mid
    )
    back_tokens = to_tokens(back_first.astype(jnp.bfloat16))
    back_rows = back_tokens.reshape(token_chans * samples, agents)
    back_hidden = project(tok_out, 0, back_rows)
    back_hidden_pre = (back_hidden * gelu_slope(hidden_pre)).astype(jnp.bfloat16)
    back_spread = (
        expand(back_hidden_pre, tok_in, 1)
        .astype(jnp.bfloat16)
        .reshape(token_chans, samples, agents)
    )
    back_norm = to_channels(back_spread)
    input_grad = back_first + norm_backward(
        back_norm.astype(jnp.float32), norm_gain, unit_in, scale_in
    )
    return (input_grad, head_grad)


def solution(mesh):
    in_specs = (
        P(None, None, ("agent", "chan", "batch")),
        P(),
        P("agent", None),
        P(None, "agent"),
        P(),
        P(),
        P(),
        P(),
        P(None, ("agent", "chan", "batch")),
        P(("agent", "chan", "batch")),
    )
    out_specs = (P(None, None, ("agent", "chan", "batch")), P())
    return jax.shard_map(shards, mesh=mesh, in_specs=in_specs, out_specs=out_specs, check_vma=False)
```

profile of v0, /device:TPU:1, one launch (start us, length us, event | category | flops | bytes accessed | tf_op | source)
XLA Modules:
  0.0 469.4 jit_solution(13224073951282337597)
XLA Ops:
  7.2 1.6 convert_reduce_fusion
  8.9 1.5 fusion.21
  10.4 0.4 fusion.16
  10.8 23.5 %all_to_all.48 = bf16[256,16,128]{2,1,0:T(8,128)(2,1)S(1)} all-to-all(bf16[256,16,128]{2,1,0:T(8,128)(2,1)S(1)} %fusion.16), channel_id=1, replica_groups=mesh['agent'=8,'chan'=8,'batch'=2] {'chan','batch'}, dimensions={0} | all-to-all | bytes 2097152 | tf_op jit(solution)/shard_map/all_to_all | solution.py:45
  34.3 0.7 copy.56
  35.0 7.0 %convolution_bitcast_fusion.1 = f32[2048,256]{0,1:T(8,128)} fusion(bf16[2048,2048]{1,0:T(8,128)(2,1)} %param.12, bf16[32,8,16,128]{3,2,1,0:T(8,128)(2,1)S(1)} %bitcast.134), kind=kOutput, calls=%fused_computation.23 | convolution fusion | flops 2147483648 | bytes 11534336 | tf_op jit(solution)/shard_map/dot_general | solution.py:54
  42.1 64.0 %all-reduce.3.cloned.1.call-done = f32[2048,256]{0,1:T(8,128)} async-done(((f32[2048,256]{0,1:T(8,128)}), f32[2048,256]{0,1:T(8,128)}) %all-reduce.3.cloned.1.call-update) | async-done | bytes 2097168 | tf_op jit(solution)/shard_map/psum | solution.py:57
  106.1 6.6 %convolution_convert_fusion.1 = bf16[256,2048]{1,0:T(8,128)(2,1)S(1)} fusion(bf16[2048,2048]{1,0:T(8,128)(2,1)} %param.13, f32[2048,256]{0,1:T(8,128)} %all-reduce.3.cloned.1.call-done), kind=kOutput, calls=%fused_computation.27 | convolution fusion | flops 2152726528 | bytes 11534336 | tf_op jit(solution)/shard_map/dot_general | solution.py:61
  112.6 8.5 %copy.57 = bf16[16,16,2048]{1,0,2:T(8,128)(2,1)} copy(bf16[16,16,2048]{2,1,0:T(8,128)(2,1)S(1)} %bitcast.133) | data formatting | bytes 2097152 | tf_op jit(solution)/shard_map/reshape | solution.py:76
  121.1 11.2 %reshape.152 = bf16[16,2,16384]{2,1,0:T(2,128)(2,1)} reshape(bf16[2048,16,16]{2,1,0:T(8,128)(2,1)} %bitcast.124) | data formatting | bytes 2097152
  132.4 6.7 %all-to-all-start.1 = ((bf16[16,2,16384]{2,1,0:T(2,128)(2,1)}), bf16[16,2,16384]{2,1,0:T(2,128)(2,1)S(1)}, u32[]{:S(2)}, u32[]{:S(2)}) async-start(bf16[16,2,16384]{2,1,0:T(2,128)(2,1)} %reshape.152), calls=%async_computation.1 | async-start | bytes 2097152 | tf_op jit(solution)/shard_map/all_to_all | solution.py:49
  139.0 0.5 all-reduce.5.cloned.1.call-start
  139.7 0.6 gather_fusion
  140.5 13.1 %all-to-all-done.1 = bf16[16,2,16384]{2,1,0:T(2,128)(2,1)S(1)} async-done(((bf16[16,2,16384]{2,1,0:T(2,128)(2,1)}), bf16[16,2,16384]{2,1,0:T(2,128)(2,1)S(1)}, u32[]{:S(2)}, u32[]{:S(2)}) %all-to-all-start.1) | async-done | bytes 1048608 | tf_op jit(solution)/shard_map/all_to_all | solution.py:49
  153.6 7.5 %reshape.153 = bf16[2048,16,16]{2,1,0:T(8,128)(2,1)} reshape(bf16[16,2,16384]{2,1,0:T(2,128)(2,1)S(1)} %all-to-all-done.1) | data formatting | bytes 2097152
  161.1 10.9 %convert_bitcast_fusion = f32[16,16,16,128]{2,1,3,0:T(8,128)} fusion(bf16[16,16,16,128]{1,0,3,2:T(8,128)(2,1)} %bitcast.123), kind=kLoop, calls=%fused_computation.1 | loop fusion | flops 524288 | bytes 3145728 | tf_op jit(solution)/shard_map/convert_element_type | solution.py:79
  172.0 11.4 %copy.58 = f32[16,16,16,128]{3,2,1,0:T(8,128)} copy(f32[16,16,16,128]{2,1,3,0:T(8,128)} %convert_bitcast_fusion) | data formatting | bytes 4194304 | tf_op jit(solution)/shard_map/convert_element_type | solution.py:79
  183.4 2.2 fusion.76
  185.6 1.8 copy.59
  187.7 0.4 copy-done.13
  188.1 0.4 multiply_convert_fusion.8
  188.5 1.3 fusion.34
  190.1 3.0 fusion.10
  193.2 0.4 fusion.77
  193.6 0.6 copy-done.8
  194.2 1.8 fusion.71
  196.0 9.5 %fusion.29 = (f32[2048]{0:T(1024)S(1)}, f32[2048,256]{1,0:T(8,128)}) fusion(f32[256]{0:T(256)S(1)} %copy-done.13, bf16[256,1024]{1,0:T(8,128)(2,1)S(1)} %copy-done, f32[2048,1024]{1,0:T(8,128)} %copy-done.6, bf16[1024,256]{1,0:T(8,128)(2,1)S(1)} %copy-done.15, f32[2048,256]{1,0:T(8,128)} %fusion.71), kind=kOutput, calls=%fused_computation.48 | convolution fusion | flops 2188376064 | bytes 13640704 | tf_op jit(solution)/shard_map/dot_general | solution.py:115
  205.5 3.1 copy.62
  208.6 3.2 copy.63
  211.8 2.1 multiply_reduce_fusion.1
  214.0 0.6 copy-done.7
  214.7 2.1 fusion.75
  216.7 17.1 %all_to_all.49 = bf16[256,16,128]{2,1,0:T(8,128)(2,1)S(1)} all-to-all(bf16[256,16,128]{2,1,0:T(8,128)(2,1)S(1)} %get-tuple-element.2), channel_id=1, replica_groups=mesh['agent'=8,'chan'=8,'batch'=2] {'chan','batch'}, dimensions={0} | all-to-all | bytes 2097152 | tf_op jit(solution)/shard_map/all_to_all | solution.py:45
  233.8 0.7 copy.64
  234.5 7.0 %convolution_bitcast_fusion = f32[2048,256]{0,1:T(8,128)} fusion(bf16[2048,2048]{1,0:T(8,128)(2,1)} %param.13, bf16[32,8,16,128]{3,2,1,0:T(8,128)(2,1)S(1)} %bitcast.135), kind=kOutput, calls=%fused_computation.22 | convolution fusion | flops 2147483648 | bytes 11534336 | tf_op jit(solution)/shard_map/dot_general | solution.py:54
  241.5 70.8 %all-reduce.5.cloned.1.call-done = f32[2048,256]{0,1:T(8,128)} async-done(((f32[2048,256]{0,1:T(8,128)}), f32[2048,256]{0,1:T(8,128)}) %all-reduce.5.cloned.1.call-update) | async-done | bytes 2097168 | tf_op jit(solution)/shard_map/psum | solution.py:57
  312.3 7.8 %convolution_convert_fusion = bf16[256,2048]{1,0:T(8,128)(2,1)S(1)} fusion(bf16[2048,2048]{1,0:T(8,128)(2,1)} %param.12, f32[2048,256]{0,1:T(8,128)} %all-reduce.5.cloned.1.call-done, f32[2048,256]{0,1:T(8,128)} %all-reduce.3.cloned.1.call-done), kind=kOutput, calls=%fused_computation.26 | convolution fusion | flops 2157969408 | bytes 13631488 | tf_op jit(solution)/shard_map/dot_general | solution.py:61
  320.1 8.5 %copy.65 = bf16[16,16,2048]{1,0,2:T(8,128)(2,1)} copy(bf16[16,16,2048]{2,1,0:T(8,128)(2,1)S(1)} %bitcast.132) | data formatting | bytes 2097152 | tf_op jit(solution)/shard_map/reshape | solution.py:128
  328.6 11.2 %reshape.154 = bf16[16,2,16384]{2,1,0:T(2,128)(2,1)} reshape(bf16[2048,16,16]{2,1,0:T(8,128)(2,1)} %bitcast.125) | data formatting | bytes 2097152
  339.9 6.7 %all-to-all-start.3 = ((bf16[16,2,16384]{2,1,0:T(2,128)(2,1)}), bf16[16,2,16384]{2,1,0:T(2,128)(2,1)S(1)}, u32[]{:S(2)}, u32[]{:S(2)}) async-start(bf16[16,2,16384]{2,1,0:T(2,128)(2,1)} %reshape.154), calls=%async_computation.3 | async-start | bytes 2097152 | tf_op jit(solution)/shard_map/all_to_all | solution.py:49
  346.9 73.3 %psum.23 = f32[256,8]{0,1:T(8,128)S(1)} all-reduce(f32[256,8]{0,1:T(8,128)S(1)} %fusion.69), channel_id=1, replica_groups=mesh['agent'=8,'chan'=8,'batch'=2] {'agent','chan','batch'}, use_global_device_ids=true, to_apply=%region_12.13 | all-reduce | flops 2048 | bytes 16384 | tf_op jit(solution)/shard_map/psum | solution.py:105
  420.2 0.6 broadcast_multiply_fusion
  420.8 7.5 %reshape.155 = bf16[2048,16,16]{2,1,0:T(8,128)(2,1)} reshape(bf16[16,2,16384]{2,1,0:T(2,128)(2,1)S(1)} %all-to-all-done.3) | data formatting | bytes 2097152
  428.3 10.9 %convert_bitcast_fusion.1 = f32[16,16,16,128]{2,1,3,0:T(8,128)} fusion(bf16[2048,16,16]{2,1,0:T(8,128)(2,1)} %reshape.155), kind=kLoop, calls=%fused_computation.2 | loop fusion | flops 524288 | bytes 3145728 | tf_op jit(solution)/shard_map/convert_element_type | solution.py:132
  439.2 5.7 %multiply_reduce_fusion = f32[16,128]{0,1:T(8,128)S(1)} fusion(f32[16,16]{1,0:T(8,128)S(1)} %mul.242, bf16[16,16,16,128]{1,0,3,2:T(8,128)(2,1)} %bitcast.122), kind=kLoop, calls=%fused_computation.3 | loop fusion | flops 1570816 | bytes 1057792 | tf_op jit(solution)/shard_map/reduce_sum | solution.py:39
  445.0 11.5 %copy.66 = f32[16,16,16,128]{3,2,1,0:T(8,128)} copy(f32[16,16,16,128]{2,1,3,0:T(8,128)} %convert_bitcast_fusion.1) | data formatting | bytes 4194304 | tf_op jit(solution)/shard_map/convert_element_type | solution.py:132
  456.5 2.2 fusion.17
  458.7 3.6 fusion.20
  (52 shorter events, 1.5 us)
Async XLA Ops:
  7.2 181.3 %copy-start = (bf16[256,1024]{1,0:T(8,128)(2,1)S(1)}, bf16[256,1024]{1,0:T(8,128)(2,1)}, u32[]{:S(2)}) copy-start(bf16[256,1024]{1,0:T(8,128)(2,1)} %param.15) | copy-start | bytes 1572868
  7.2 3.2 copy-start.2
  7.2 3.2 copy-start.12
  7.2 98.9 %all-reduce.3.cloned.1.call-start = ((), (), s32[]{:S(2)}) async-start(), calls=%async_computation.4 | async-start | bytes 4194304 | tf_op jit(solution)/shard_map/psum | solution.py:57
  132.4 7.2 %copy-start.14 = (s32[16,128]{1,0:T(8,128)S(1)}, s32[16,128]{1,0:T(8,128)}, u32[]{:S(2)}) copy-start(s32[16,128]{1,0:T(8,128)} %param.18) | copy-start | bytes 24580
  132.4 7.3 %copy-start.16 = (s32[128]{0:T(128)S(1)}, s32[128]{0:T(128)}, u32[]{:S(2)}) copy-start(s32[128]{0:T(128)} %param.19) | copy-start | bytes 1540
  132.4 21.2 %all-to-all-start.1 = ((bf16[16,2,16384]{2,1,0:T(2,128)(2,1)}), bf16[16,2,16384]{2,1,0:T(2,128)(2,1)S(1)}, u32[]{:S(2)}, u32[]{:S(2)}) async-start(bf16[16,2,16384]{2,1,0:T(2,128)(2,1)} %reshape.152), calls=%async_computation.1 | async-start | bytes 2097152 | tf_op jit(solution)/shard_map/all_to_all | solution.py:49
  139.0 173.2 %all-reduce.5.cloned.1.call-start = ((), (), s32[]{:S(2)}) async-start(), calls=%async_computation.5 | async-start | bytes 4194304 | tf_op jit(solution)/shard_map/psum | solution.py:57
  187.4 0.7 copy-start.13
  188.4 1.6 copy-start.10
  188.5 1.7 copy-start.15
  189.8 3.3 copy-start.6
  190.1 3.0 copy-start.11
  193.2 1.0 copy-start.8
  211.8 2.2 copy-start.4
  211.8 2.8 copy-start.7
  339.9 6.7 %copy-start.9 = (bf16[256,2048]{0,1:T(8,128)(2,1)S(1)}, bf16[256,2048]{0,1:T(8,128)(2,1)}, u32[]{:S(2)}) copy-start(bf16[256,2048]{0,1:T(8,128)(2,1)} %copy-done.8) | copy-start | bytes 3145732
  339.9 80.9 %all-to-all-start.3 = ((bf16[16,2,16384]{2,1,0:T(2,128)(2,1)}), bf16[16,2,16384]{2,1,0:T(2,128)(2,1)S(1)}, u32[]{:S(2)}, u32[]{:S(2)}) async-start(bf16[16,2,16384]{2,1,0:T(2,128)(2,1)} %reshape.154), calls=%async_computation.3 | async-start | bytes 2097152 | tf_op jit(solution)/shard_map/all_to_all | solution.py:49
  444.9 11.5 %copy-start.3 = (bf16[256,16,128]{2,1,0:T(8,128)(2,1)S(1)}, bf16[256,16,128]{2,1,0:T(8,128)(2,1)}, u32[]{:S(2)}) copy-start(bf16[256,16,128]{2,1,0:T(8,128)(2,1)} %param.10) | copy-start | bytes 3145732
  456.5 2.2 copy-start.5
  458.7 3.6 copy-start.1
Sparse Core Ops, SparseCore 0:
  42.2 63.8 all-reduce.2
  241.7 70.5 all-reduce.4
where the time goes:
time: 477 us; the launch traced here: 469 us
  waiting for transfers between devices  148 us (31%)
  blocking collectives  114 us (24%)
  local copies, waits for them, and re-layouts  89.9 us (19%)
  matrix products  44.8 us (9%)
  other arithmetic  44.6 us (9%)
  between operations  14.6 us (3%)
  starting transfers between devices  13.9 us (3%)
    psum x2, waiting for transfers between devices, project(): return lax.psum(partial_sum, 'agent')  135 us
    psum x1, blocking collectives, shards(): head_total = lax.psum(head_part, ('agent', 'chan', 'batch'))  73.3 us
    all_to_all x2, blocking collectives, to_tokens(): lax.all_to_all(field, ('chan', 'batch'), split_axis=0, concat_axis=2, til...  40.6 us
    unnamed x39, local copies, waits for them, and re-layouts  39.6 us
    dot_general x2, matrix products, expand(): lax.dot_general(spread, weight, (((0,), (hidden_dim,)), ((), ())), prefer...  14.4 us
    dot_general x2, matrix products, project(): lax.dot_general(weight, rows, (((agent_dim,), (1,)), ((), ())), preferred...  14.1 us
    all_to_all x2, starting transfers between devices, to_channels(): lax.all_to_all(field, ('chan', 'batch'), split_axis=2, concat_axis=0, til...  13.3 us
    all_to_all x2, waiting for transfers between devices, to_channels(): lax.all_to_all(field, ('chan', 'batch'), split_axis=2, concat_axis=0, til...  13.1 us
  transfers between devices with their start and end apart: 4, of which 3 were waited for; matrix products, arithmetic and copies ran while one was open for 0% of the time, Pallas kernels for 0%

commit v1 on v0

--- a/solution.py
+++ b/solution.py
@@ -54,7 +54,7 @@
     partial_sum = lax.dot_general(
         weight, rows, (((agent_dim,), (1,)), ((), ())), preferred_element_type=jnp.float32
     )
-    return lax.psum(partial_sum, "agent")
+    return jnp.sum(lax.all_gather(partial_sum, "agent"), axis=0)
 
 
 def expand(spread, weight, hidden_dim):

time: 477 us -> 564 us (1.18)
  waiting for transfers between devices: 148 us -> 185 us
  local copies, waits for them, and re-layouts: 89.9 us -> 125 us
  other arithmetic: 44.6 us -> 57.9 us
    all_gather x0 -> x2, waiting for transfers between devices: none -> 169 us  [project(): return jnp.sum(lax.all_gather(partial_sum, 'agent'), axis=0)]
    psum x2 -> x0, waiting for transfers between devices: 135 us -> none  [project(): return lax.psum(partial_sum, 'agent')]
    unnamed x39, local copies, waits for them, and re-layouts: 39.6 us -> 74.1 us
    reduce_sum x0 -> x2, other arithmetic: none -> 10.8 us  [project(): return jnp.sum(lax.all_gather(partial_sum, 'agent'), axis=0)]
where the time goes in v1:
time: 564 us; the launch traced here: 553 us
  waiting for transfers between devices  185 us (33%)
  local copies, waits for them, and re-layouts  125 us (22%)
  blocking collectives  114 us (20%)
  other arithmetic  57.9 us (10%)
  matrix products  43.7 us (8%)
  between operations  14.8 us (3%)
  starting transfers between devices  13.4 us (2%)
    all_gather x2, waiting for transfers between devices, project(): return jnp.sum(lax.all_gather(partial_sum, 'agent'), axis=0)  169 us
    unnamed x39, local copies, waits for them, and re-layouts  74.1 us
    psum x1, blocking collectives, shards(): head_total = lax.psum(head_part, ('agent', 'chan', 'batch'))  70 us
    all_to_all x2, blocking collectives, to_tokens(): lax.all_to_all(field, ('chan', 'batch'), split_axis=0, concat_axis=2, til...  44 us
    all_to_all x2, waiting for transfers between devices, to_channels(): lax.all_to_all(field, ('chan', 'batch'), split_axis=2, concat_axis=0, til...  15.5 us
    dot_general x2, matrix products, project(): lax.dot_general(weight, rows, (((agent_dim,), (1,)), ((), ())), preferred...  14.1 us
    all_to_all x2, starting transfers between devices, to_channels(): lax.all_to_all(field, ('chan', 'batch'), split_axis=2, concat_axis=0, til...  13.3 us
    dot_general x2, matrix products, expand(): lax.dot_general(spread, weight, (((0,), (hidden_dim,)), ((), ())), prefer...  13.2 us
  transfers between devices with their start and end apart: 4, of which 3 were waited for; matrix products, arithmetic and copies ran while one was open for 0% of the time, Pallas kernels for 0%

profile of v1, /device:TPU:1, one launch (start us, length us, event | category | flops | bytes accessed | tf_op | source)
XLA Modules:
  0.0 553.2 jit_solution(3151494967753518563)
XLA Ops:
  7.2 1.6 convert_reduce_fusion
  8.9 1.5 fusion.21
  10.4 0.4 fusion.16
  10.8 23.5 %all_to_all.48 = bf16[256,16,128]{2,1,0:T(8,128)(2,1)S(1)} all-to-all(bf16[256,16,128]{2,1,0:T(8,128)(2,1)S(1)} %fusion.16), channel_id=1, replica_groups=mesh['agent'=8,'chan'=8,'batch'=2] {'chan','batch'}, dimensions={0} | all-to-all | bytes 2097152 | tf_op jit(solution)/shard_map/all_to_all | solution.py:45
  34.3 0.7 copy.56
  35.0 7.0 %convolution_bitcast_fusion.1 = f32[2048,256]{0,1:T(8,128)} fusion(bf16[2048,2048]{1,0:T(8,128)(2,1)} %param.12, bf16[32,8,16,128]{3,2,1,0:T(8,128)(2,1)S(1)} %bitcast.146), kind=kOutput, calls=%fused_computation.25 | convolution fusion | flops 2147483648 | bytes 11534336 | tf_op jit(solution)/shard_map/dot_general | solution.py:54
  42.1 85.5 %all-gather.5.cloned.1.call-done = f32[16384,256]{0,1:T(8,128)} async-done(((f32[2048,256]{0,1:T(8,128)}), f32[16384,256]{0,1:T(8,128)}) %all-gather.5.cloned.1.call-update) | async-done | bytes 16777232 | tf_op jit(solution)/shard_map/all_gather | solution.py:57
  127.6 17.6 %copy.69 = f32[32,8,8,2048]{3,2,1,0:T(8,128)S(1)} copy(f32[32,8,8,2048]{3,1,2,0:T(8,128)} %bitcast.136) | data formatting | bytes 33554432
  145.2 5.4 bitcast_reduce_fusion.1
  150.6 6.7 %convolution_convert_fusion.1 = bf16[256,2048]{1,0:T(8,128)(2,1)S(1)} fusion(bf16[2048,2048]{1,0:T(8,128)(2,1)} %param.13, f32[2048,256]{0,1:T(8,128)S(1)} %bitcast_reduce_fusion.1), kind=kOutput, calls=%fused_computation.29 | convolution fusion | flops 2152726528 | bytes 11534336 | tf_op jit(solution)/shard_map/dot_general | solution.py:61
  157.3 8.5 %copy.57 = bf16[16,16,2048]{1,0,2:T(8,128)(2,1)} copy(bf16[16,16,2048]{2,1,0:T(8,128)(2,1)S(1)} %bitcast.145) | data formatting | bytes 2097152 | tf_op jit(solution)/shard_map/reshape | solution.py:76
  165.8 11.2 %reshape.154 = bf16[16,2,16384]{2,1,0:T(2,128)(2,1)} reshape(bf16[2048,16,16]{2,1,0:T(8,128)(2,1)} %bitcast.134) | data formatting | bytes 2097152
  177.0 6.7 %all-to-all-start.1 = ((bf16[16,2,16384]{2,1,0:T(2,128)(2,1)}), bf16[16,2,16384]{2,1,0:T(2,128)(2,1)S(1)}, u32[]{:S(2)}, u32[]{:S(2)}) async-start(bf16[16,2,16384]{2,1,0:T(2,128)(2,1)} %reshape.154), calls=%async_computation.1 | async-start | bytes 2097152 | tf_op jit(solution)/shard_map/all_to_all | solution.py:49
  183.9 0.6 gather_fusion
  184.7 15.5 %all-to-all-done.1 = bf16[16,2,16384]{2,1,0:T(2,128)(2,1)S(1)} async-done(((bf16[16,2,16384]{2,1,0:T(2,128)(2,1)}), bf16[16,2,16384]{2,1,0:T(2,128)(2,1)S(1)}, u32[]{:S(2)}, u32[]{:S(2)}) %all-to-all-start.1) | async-done | bytes 1048608 | tf_op jit(solution)/shard_map/all_to_all | solution.py:49
  200.2 7.5 %reshape.155 = bf16[2048,16,16]{2,1,0:T(8,128)(2,1)} reshape(bf16[16,2,16384]{2,1,0:T(2,128)(2,1)S(1)} %all-to-all-done.1) | data formatting | bytes 2097152
  207.7 10.9 %convert_bitcast_fusion = f32[16,16,16,128]{2,1,3,0:T(8,128)} fusion(bf16[16,16,16,128]{1,0,3,2:T(8,128)(2,1)} %bitcast.133), kind=kLoop, calls=%fused_computation.3 | loop fusion | flops 524288 | bytes 3145728 | tf_op jit(solution)/shard_map/convert_element_type | solution.py:79
  218.6 11.4 %copy.58 = f32[16,16,16,128]{3,2,1,0:T(8,128)} copy(f32[16,16,16,128]{2,1,3,0:T(8,128)} %convert_bitcast_fusion) | data formatting | bytes 4194304 | tf_op jit(solution)/shard_map/convert_element_type | solution.py:79
  230.0 2.2 fusion.76
  232.2 1.8 copy.59
  235.1 1.3 fusion.34
  236.8 3.0 fusion.10
  239.8 0.4 fusion.77
  240.2 0.6 copy-done.5
  240.8 1.8 fusion.71
  242.6 9.5 %fusion.29 = (f32[2048]{0:T(1024)S(1)}, f32[2048,256]{1,0:T(8,128)}) fusion(f32[256]{0:T(256)S(1)} %copy-done.12, bf16[256,1024]{1,0:T(8,128)(2,1)S(1)} %copy-done, f32[2048,1024]{1,0:T(8,128)} %copy-done.4, bf16[1024,256]{1,0:T(8,128)(2,1)S(1)} %copy-done.14, f32[2048,256]{1,0:T(8,128)} %fusion.71), kind=kOutput, calls=%fused_computation.50 | convolution fusion | flops 2188376064 | bytes 13640704 | tf_op jit(solution)/shard_map/dot_general | solution.py:115
  252.2 3.1 copy.62
  255.3 2.0 multiply_reduce_fusion.1
  257.3 3.2 copy.63
  260.5 4.2 fusion.75
  264.7 20.5 %all_to_all.49 = bf16[256,16,128]{2,1,0:T(8,128)(2,1)S(1)} all-to-all(bf16[256,16,128]{2,1,0:T(8,128)(2,1)S(1)} %get-tuple-element.2), channel_id=1, replica_groups=mesh['agent'=8,'chan'=8,'batch'=2] {'chan','batch'}, dimensions={0} | all-to-all | bytes 2097152 | tf_op jit(solution)/shard_map/all_to_all | solution.py:45
  285.2 0.7 copy.64
  285.9 7.1 %convolution_bitcast_fusion = f32[2048,256]{0,1:T(8,128)} fusion(bf16[2048,2048]{1,0:T(8,128)(2,1)} %param.13, bf16[32,8,16,128]{3,2,1,0:T(8,128)(2,1)S(1)} %bitcast.147), kind=kOutput, calls=%fused_computation.24 | convolution fusion | flops 2147483648 | bytes 11534336 | tf_op jit(solution)/shard_map/dot_general | solution.py:54
  293.0 83.8 %all-gather.7.cloned.1.call-done = f32[16384,256]{0,1:T(8,128)} async-done(((f32[2048,256]{0,1:T(8,128)}), f32[16384,256]{0,1:T(8,128)}) %all-gather.7.cloned.1.call-update) | async-done | bytes 16777232 | tf_op jit(solution)/shard_map/all_gather | solution.py:57
  376.8 17.6 %copy.72 = f32[32,8,8,2048]{3,2,1,0:T(8,128)S(1)} copy(f32[32,8,8,2048]{3,1,2,0:T(8,128)} %bitcast.137) | data formatting | bytes 33554432
  394.4 5.4 bitcast_reduce_fusion
  399.8 6.6 %convolution_convert_fusion = bf16[256,2048]{1,0:T(8,128)(2,1)S(1)} fusion(bf16[2048,2048]{1,0:T(8,128)(2,1)} %param.12, f32[2048,256]{0,1:T(8,128)S(1)} %bitcast_reduce_fusion, f32[2048,256]{0,1:T(8,128)S(1)} %copy-done.8), kind=kOutput, calls=%fused_computation.28 | convolution fusion | flops 2157969408 | bytes 13631488 | tf_op jit(solution)/shard_map/dot_general | solution.py:61
  406.4 8.8 %copy.65 = bf16[16,16,2048]{1,0,2:T(8,128)(2,1)} copy(bf16[16,16,2048]{2,1,0:T(8,128)(2,1)S(1)} %bitcast.144) | data formatting | bytes 2097152 | tf_op jit(solution)/shard_map/reshape | solution.py:128
  415.1 11.2 %reshape.156 = bf16[16,2,16384]{2,1,0:T(2,128)(2,1)} reshape(bf16[2048,16,16]{2,1,0:T(8,128)(2,1)} %bitcast.135) | data formatting | bytes 2097152
  426.4 6.7 %all-to-all-start.3 = ((bf16[16,2,16384]{2,1,0:T(2,128)(2,1)}), bf16[16,2,16384]{2,1,0:T(2,128)(2,1)S(1)}, u32[]{:S(2)}, u32[]{:S(2)}) async-start(bf16[16,2,16384]{2,1,0:T(2,128)(2,1)} %reshape.156), calls=%async_computation.3 | async-start | bytes 2097152 | tf_op jit(solution)/shard_map/all_to_all | solution.py:49
  433.4 70.0 %psum.7 = f32[256,8]{0,1:T(8,128)S(1)} all-reduce(f32[256,8]{0,1:T(8,128)S(1)} %fusion.69), channel_id=1, replica_groups=mesh['agent'=8,'chan'=8,'batch'=2] {'agent','chan','batch'}, use_global_device_ids=true, to_apply=%region_12.13 | all-reduce | flops 2048 | bytes 16384 | tf_op jit(solution)/shard_map/psum | solution.py:105
  503.4 0.6 broadcast_multiply_fusion
  504.0 7.5 %reshape.157 = bf16[2048,16,16]{2,1,0:T(8,128)(2,1)} reshape(bf16[16,2,16384]{2,1,0:T(2,128)(2,1)S(1)} %all-to-all-done.3) | data formatting | bytes 2097152
  511.5 10.9 %convert_bitcast_fusion.1 = f32[16,16,16,128]{2,1,3,0:T(8,128)} fusion(bf16[2048,16,16]{2,1,0:T(8,128)(2,1)} %reshape.157), kind=kLoop, calls=%fused_computation.4 | loop fusion | flops 524288 | bytes 3145728 | tf_op jit(solution)/shard_map/convert_element_type | solution.py:132
  522.4 11.5 %copy.66 = f32[16,16,16,128]{3,2,1,0:T(8,128)} copy(f32[16,16,16,128]{2,1,3,0:T(8,128)} %convert_bitcast_fusion.1) | data formatting | bytes 4194304 | tf_op jit(solution)/shard_map/convert_element_type | solution.py:132
  533.9 2.0 fusion.17
  535.9 5.7 %multiply_reduce_fusion = f32[16,128]{0,1:T(8,128)S(1)} fusion(f32[16,16]{1,0:T(8,128)S(1)} %mul.242, bf16[16,16,16,128]{1,0,3,2:T(8,128)(2,1)} %bitcast.132), kind=kLoop, calls=%fused_computation.5 | loop fusion | flops 1570816 | bytes 1057792 | tf_op jit(solution)/shard_map/reduce_sum | solution.py:39
  541.7 4.3 fusion.20
  (54 shorter events, 2.2 us)
Async XLA Ops:
  7.2 227.9 %copy-start = (bf16[256,1024]{1,0:T(8,128)(2,1)S(1)}, bf16[256,1024]{1,0:T(8,128)(2,1)}, u32[]{:S(2)}) copy-start(bf16[256,1024]{1,0:T(8,128)(2,1)} %param.15) | copy-start | bytes 1572868
  7.2 3.2 copy-start.2
  7.2 3.2 copy-start.11
  7.2 120.4 %all-gather.5.cloned.1.call-start = ((), (), s32[]{:S(2)}) async-start(), calls=%async_computation.4 | async-start | bytes 18874368 | tf_op jit(solution)/shard_map/all_gather | solution.py:57
  150.6 6.7 %copy-start.7 = (f32[2048,256]{0,1:T(8,128)}, f32[2048,256]{0,1:T(8,128)S(1)}, u32[]{:S(2)}) copy-start(f32[2048,256]{0,1:T(8,128)S(1)} %bitcast_reduce_fusion.1) | copy-start | bytes 6291460
  177.0 6.7 %copy-start.13 = (s32[16,128]{1,0:T(8,128)S(1)}, s32[16,128]{1,0:T(8,128)}, u32[]{:S(2)}) copy-start(s32[16,128]{1,0:T(8,128)} %param.18) | copy-start | bytes 24580
  177.0 6.8 %copy-start.15 = (s32[128]{0:T(128)S(1)}, s32[128]{0:T(128)}, u32[]{:S(2)}) copy-start(s32[128]{0:T(128)} %param.19) | copy-start | bytes 1540
  177.0 23.2 %all-to-all-start.1 = ((bf16[16,2,16384]{2,1,0:T(2,128)(2,1)}), bf16[16,2,16384]{2,1,0:T(2,128)(2,1)S(1)}, u32[]{:S(2)}, u32[]{:S(2)}) async-start(bf16[16,2,16384]{2,1,0:T(2,128)(2,1)} %reshape.154), calls=%async_computation.1 | async-start | bytes 2097152 | tf_op jit(solution)/shard_map/all_to_all | solution.py:49
  183.7 193.1 %all-gather.7.cloned.1.call-start = ((), (), s32[]{:S(2)}) async-start(), calls=%async_computation.5 | async-start | bytes 18874368 | tf_op jit(solution)/shard_map/all_gather | solution.py:57
  234.0 0.7 copy-start.12
  235.1 1.6 copy-start.9
  235.1 1.7 copy-start.14
  236.5 3.3 copy-start.4
  236.8 3.0 copy-start.10
  239.8 1.0 copy-start.5
  394.4 5.4 copy-start.8
  426.4 6.7 %copy-start.6 = (bf16[256,2048]{0,1:T(8,128)(2,1)S(1)}, bf16[256,2048]{0,1:T(8,128)(2,1)}, u32[]{:S(2)}) copy-start(bf16[256,2048]{0,1:T(8,128)(2,1)} %copy-done.5) | copy-start | bytes 3145732
  426.4 77.6 %all-to-all-start.3 = ((bf16[16,2,16384]{2,1,0:T(2,128)(2,1)}), bf16[16,2,16384]{2,1,0:T(2,128)(2,1)S(1)}, u32[]{:S(2)}, u32[]{:S(2)}) async-start(bf16[16,2,16384]{2,1,0:T(2,128)(2,1)} %reshape.156), calls=%async_computation.3 | async-start | bytes 2097152 | tf_op jit(solution)/shard_map/all_to_all | solution.py:49
  522.4 11.5 %copy-start.3 = (bf16[256,16,128]{2,1,0:T(8,128)(2,1)S(1)}, bf16[256,16,128]{2,1,0:T(8,128)(2,1)}, u32[]{:S(2)}) copy-start(bf16[256,16,128]{2,1,0:T(8,128)(2,1)} %param.10) | copy-start | bytes 3145732
  541.7 4.3 copy-start.1
Sparse Core Ops, SparseCore 0:
  42.2 85.3 all-gather.4
  293.1 83.6 all-gather.6
